TPU v7x, 768 devices: a whole 4x8x12 slice. The times are simulated.
768 devices in a mesh: dp: 48 (over z_lo, x, core), grp: 16 (over y, z_hi).
Axes of the slice: x: 4, y: 8, z: 12 (z_hi: 2, z_lo: 6; z = z_hi * 6 + z_lo), core: 2. Of those that a mesh axis runs over, the one named last changes fastest.
Arguments:
- embeddings: bfloat16 [294912, 512], P(('dp', 'grp')), may hold values from -0.31 to 0.31
- order: int32 [768, 384], P(('dp', 'grp')), may hold values from 0 to 383, as said below
Outputs:
- emb_grad: bfloat16 [294912, 512], P(('dp', 'grp'))
- row_loss: float32 [768, 384], P(('dp', 'grp'))
Inputs may be any that keep to these rules, and one draw needn't show every extreme that they name: Each row of order is a permutation of 0 .. 383.
All inputs are finite; a program needn't handle non-finite values.
Results may differ from a plain program's by a relative error of at most 0.0046.
Values may be sent and summed in bfloat16 or wider, within the bound.
No kernel may reach another device: no remote copies, remote signals or barrier semaphores. Data moves between devices by JAX's collectives and lax.ppermute only.
A program may use at most 32 MiB of HBM per device.

v0:
```python
import jax
import jax.numpy as jnp
from jax import lax
from jax.experimental import pallas as pl
from jax.experimental.pallas import tpu as pltpu
from jax.sharding import Mesh
from jax.sharding import PartitionSpec as P


K = 16
gamma = 16.0
F32 = jnp.float32
BF16 = jnp.bfloat16
WHERE = ("zl", "x", "zh")
LIMIT = 20 * 2**20


def rows_by_rows(a, b):
    return lax.dot_general(a, b, (((1,), (1,)), ((), ())), preferred_element_type=F32)


def chip_rows(own, sib):
    half = own.shape[0] // 2
    return jnp.concatenate([own[0:half], sib[0:half], own[half:], sib[half:]], axis=0)


def as_row(column):
    return jnp.broadcast_to(column, (column.shape[0], 128)).T[0:1]


def over_rows(value):
    return jnp.sum(value, axis=0, keepdims=True)


def over_columns(value):
    return jnp.sum(value, axis=1, keepdims=True)


def arrived_rows(order_ref):
    rows = order_ref.shape[1]
    half = rows // 2
    i = lax.broadcasted_iota(jnp.int32, (rows, rows), 0)
    source = jnp.where(i < half, 0, 1)
    i = i - source * half
    return (i // 8) * 16 + source * 8 + i % 8 == order_ref[...]


def classes_kernel(core_ref, o0_ref, o1_ref, o2_ref, sign_ref):
    core = core_ref[0]
    rows = o0_ref.shape[1]
    slot = lax.broadcasted_iota(jnp.int32, (rows, 128), 0) // K
    table = jnp.where(lax.broadcasted_iota(jnp.int32, (rows, 128), 1) == slot, 1.0, 0.0)
    table = table.astype(BF16)
    diagonal = lax.broadcasted_iota(jnp.int32, (rows, rows), 0) == lax.broadcasted_iota(
        jnp.int32, (rows, rows), 1
    )

    def fill(b, ref):
        chosen = jnp.where(arrived_rows(ref), 1.0, 0.0).astype(BF16)
        hot = jnp.dot(chosen, table, preferred_element_type=F32).astype(BF16)
        sign_ref[b] = jnp.where(diagonal, 0.0, 1.0 - 2.0 * rows_by_rows(hot, hot))

    fill(0, o0_ref)
    fill(1, o1_ref)

    @pl.when(core == 1)
    def _():
        fill(2, o2_ref)


def pack_kernel(core_ref, x_ref, full_ref, one_ref, two_ref):
    core = core_ref[0]
    half = one_ref.shape[0]
    for which in range(2):
        x = x_ref[:, which].astype(F32).reshape(half, x_ref.shape[-1])
        inv = lax.rsqrt(jnp.sum(x * x, axis=1, keepdims=True) + 1e-06)
        unit = (x * inv).astype(BF16)
        full_ref[which * half : (which + 1) * half] = unit

        @pl.when(core == 1 - which)
        def _():
            one_ref[...] = unit

        @pl.when(core == which)
        def _():
            two_ref[...] = unit


def relay_kernel(own_ref, n1a_ref, n2a_ref, out_ref, both_ref):
    half = n1a_ref.shape[0]
    rows = 2 * half
    out_ref[0:half] = n2a_ref[...]
    out_ref[half:] = n1a_ref[...]
    both_ref[0:rows] = own_ref[...]
    both_ref[rows : rows + half] = n2a_ref[...]
    both_ref[rows + half :] = n1a_ref[...]


def signed_exp(sign, sim):
    e = jnp.exp(gamma * sign * sim)
    return e, jnp.where(sign < 0.0, e, 0.0), jnp.where(sign > 0.0, e, 0.0)


def factors(pos_sum, neg_sum):
    product = pos_sum * neg_sum
    weight = product / (1.0 + product)
    return gamma * weight / neg_sum, gamma * weight / pos_sum, jnp.log(1.0 + product)


def scaled_dot(scale, e, rows):
    return jnp.dot((scale * e).astype(BF16), rows, preferred_element_type=F32)


def paired(sign, up, down, row_up, row_down, e):
    scale = jnp.where(sign < 0.0, -(down + row_down), 0.0)
    return (jnp.where(sign > 0.0, up + row_up, scale) * e).astype(BF16)


def split_store(b, total, keep_ref, send_ref):
    half = total.shape[0] // 2
    keep_ref[b * half : (b + 1) * half] = total[0:half]
    send_ref[b * half : (b + 1) * half] = total[half:]


def early_kernel(
    core_ref, own_ref, both_ref, n1a_ref, n2a_ref, n1b_ref, n2b_ref, sign_ref, o1_ref,
    e_ref, d_ref, sums_ref, acc_ref, keep_ref, send_ref,
):
    core = core_ref[0]
    rows = own_ref.shape[0]
    a, b = slice(0, rows), slice(rows, 2 * rows)
    chip = chip_rows(own_ref[...], both_ref[0:rows])
    near = jnp.concatenate([n2b_ref[...], n1b_ref[...], n2a_ref[...], n1a_ref[...]], axis=0)

    @pl.when(core == 0)
    def _():
        e_b = jnp.exp(gamma * rows_by_rows(chip[b], near))
        d_ba = jnp.exp(gamma * rows_by_rows(chip[b], chip[a]))
        sign = sign_ref[1]
        d_bb, pos, neg = signed_exp(sign, rows_by_rows(chip[b], chip[b]))
        neg_sum = over_columns(e_b) + over_columns(d_ba) + over_columns(neg)
        up, down, loss = factors(over_columns(pos), neg_sum)
        row_up = as_row(up)
        send_ref[rows : rows + 1, 0:rows] = over_rows(jnp.where(arrived_rows(o1_ref), loss, 0.0))
        coef = paired(sign, up, down, row_up, as_row(down), d_bb)
        total = jnp.dot(coef, chip[b], preferred_element_type=F32)
        total = total + scaled_dot(up, e_b, near) + scaled_dot(up, d_ba, chip[a])
        split_store(1, total, keep_ref, send_ref)

        d_ab = jnp.exp(gamma * rows_by_rows(chip[a], chip[b]))
        acc_ref[...] = scaled_dot(row_up, d_ab, chip[b])
        e_a = jnp.exp(gamma * rows_by_rows(chip[a], near))
        e_ref[a] = e_a
        d_aa, pos, neg = signed_exp(sign_ref[0], rows_by_rows(chip[a], chip[a]))
        d_ref[...] = d_aa
        sums_ref[:, 0:1] = over_columns(pos)
        sums_ref[:, 1:2] = over_columns(e_a) + over_columns(neg)

    @pl.when(core == 1)
    def _():
        scale = []
        for part, third, sign in ((a, near[b], sign_ref[0]), (b, both_ref[rows:], sign_ref[1])):
            anchors = near[part]
            e = jnp.exp(gamma * rows_by_rows(chip, anchors))
            e_ref[:, part] = e
            _, pos, neg = signed_exp(sign, rows_by_rows(anchors, anchors))
            others = jnp.exp(gamma * rows_by_rows(third, anchors))
            up, _, _ = factors(over_rows(pos), over_rows(e) + over_rows(neg) + over_rows(others))
            scale.append(up)
        scale = jnp.concatenate(scale, axis=1)
        split_store(0, scaled_dot(scale, e_ref[a], near), keep_ref, send_ref)
        acc_ref[...] = scaled_dot(scale, e_ref[b], near)


def late_kernel(
    core_ref, own_ref, both_ref, n1a_ref, n2a_ref, n1b_ref, n2b_ref, far_ref, sign_ref,
    e_ref, d_ref, sums_ref, acc_ref, o0_ref, keep_in, send_in, keep_ref, send_ref, loss_ref,
):
    core = core_ref[0]
    rows = own_ref.shape[0]
    a, b = slice(0, rows), slice(rows, 2 * rows)
    chip = chip_rows(own_ref[...], both_ref[0:rows])
    near = jnp.concatenate([n2b_ref[...], n1b_ref[...], n2a_ref[...], n1a_ref[...]], axis=0)
    far = far_ref[...]

    @pl.when(core == 0)
    def _():
        f = jnp.exp(gamma * rows_by_rows(chip[a], far))
        up, down, loss = factors(sums_ref[:, 0:1], sums_ref[:, 1:2] + over_columns(f))
        coef = paired(sign_ref[0], up, down, as_row(up), as_row(down), d_ref[...])
        total = acc_ref[...] + jnp.dot(coef, chip[a], preferred_element_type=F32)
        total = total + scaled_dot(up, e_ref[a], near) + scaled_dot(up, f, far)
        split_store(0, total, keep_ref, send_ref)
        loss_ref[...] = over_rows(jnp.where(arrived_rows(o0_ref), loss, 0.0))

    @pl.when(core == 1)
    def _():
        f = jnp.exp(gamma * rows_by_rows(chip[b], far))
        _, pos, neg = signed_exp(sign_ref[2], rows_by_rows(far, far))
        others = jnp.exp(gamma * rows_by_rows(near, far))
        up, _, _ = factors(over_rows(pos), over_rows(f) + over_rows(neg) + over_rows(others))
        split_store(1, acc_ref[...] + scaled_dot(up, f, far), keep_ref, send_ref)
        loss_ref[...] = jnp.zeros_like(loss_ref)


def final_kernel(core_ref, x_ref, keep_ref, other_ref, losses_ref, grad_ref, loss_ref):
    rows = keep_ref.shape[0]
    loss_ref[...] = jnp.where(
        core_ref[0] == 0, losses_ref[...], other_ref[rows : rows + 1, 0:rows]
    )
    features = x_ref.shape[-1]
    half = keep_ref.shape[0] // 2
    for which in range(2):
        part = slice(which * half, (which + 1) * half)
        total = keep_ref[part] + other_ref[part]
        x = x_ref[:, which].astype(F32).reshape(half, features)
        inv = lax.rsqrt(jnp.sum(x * x, axis=1, keepdims=True) + 1e-06)
        u = x * inv
        grad = (total - u * jnp.sum(u * total, axis=1, keepdims=True)) * inv
        grad_ref[:, which] = grad.reshape(half // 8, 8, features).astype(BF16)


def copy_kernel(x_ref, out_ref):
    out_ref[...] = x_ref[...]


VMEM = pl.BlockSpec(memory_space=pltpu.VMEM)
SMEM = pl.BlockSpec(memory_space=pltpu.SMEM)


def shape(*size, dtype=F32):
    return jax.ShapeDtypeStruct(size, dtype)


def call(kernel, inputs, outputs, work, aliases=None):
    return pl.pallas_call(
        kernel,
        out_shape=outputs,
        in_specs=[SMEM if a.ndim == 1 else VMEM for a in inputs],
        out_specs=jax.tree.map(lambda _: VMEM, outputs),
        input_output_aliases=aliases or {},
        compiler_params=pltpu.CompilerParams(vmem_limit_bytes=LIMIT),
        cost_estimate=pl.CostEstimate(
            flops=int(work * 10**9), bytes_accessed=10**5, transcendentals=0
        ),
    )(*inputs)


def on_device(embeddings, order):
    rows, features = embeddings.shape
    peers = lax.axis_size(WHERE)
    per_peer = rows // peers
    half = rows // 2
    core = lax.axis_index("c").astype(jnp.int32).reshape(1)
    ring = lax.axis_size("y")

    def fetch_order(moves):
        route = [
            ((c * ring + y) * 2 + h, (core * ring + (y + s) % ring) * 2 + c)
            for h, core, s in moves
            for c in range(2)
            for y in range(ring)
        ]
        return lax.ppermute(order, ("c", "y", "zh"), route)

    def along(value, moves):
        route = [(a * ring + y, b * ring + (y + s) % ring) for a, b, s in moves for y in range(ring)]
        return lax.ppermute(value, ("c", "y"), route)

    o0 = fetch_order(((0, 0, 0), (1, 1, -1)))
    o1 = fetch_order(((1, 0, 0), (0, 1, -1)))
    o2 = fetch_order(((0, 1, -2),))
    arrived = lax.all_to_all(
        embeddings.reshape(peers, per_peer, features), WHERE, 0, 0, tiled=True
    ).reshape(peers // 2, 2, per_peer, features)
    block = shape(rows, features, dtype=BF16)
    half_block = shape(half, features, dtype=BF16)

    own, one, two = call(pack_kernel, (core, arrived), (block, half_block, half_block), 0.01)
    straight = ((0, 0, 1), (1, 1, -1))
    across = ((1, 0, 1), (0, 1, -1))
    n1a = along(one, straight)
    n2a = along(two, across)
    n1b = along(two, straight)
    n2b = along(one, across)
    near = (n1a, n2a, n1b, n2b)
    relay, both = call(
        relay_kernel, (own, n1a, n2a), (block, shape(2 * rows, features, dtype=BF16)), 0.01
    )
    far = along(relay, straight)
    sib = along(both, ((0, 1, 0), (1, 0, 0)))

    sign = call(classes_kernel, (core, o0, o1, o2), shape(3, rows, rows), 0.5)
    half_grads = (shape(rows, features), shape(rows + 8, features))
    e, d, sums, acc, keep, send = call(
        early_kernel,
        (core, own, sib, *near, sign, o1),
        (
            shape(2 * rows, 2 * rows),
            shape(rows, rows),
            shape(rows, 8),
            shape(rows, features),
            *half_grads,
        ),
        2.0,
    )
    keep, send, losses = call(
        late_kernel,
        (core, own, sib, *near, far, sign, e, d, sums, acc, o0, keep, send),
        (*half_grads, shape(1, rows)),
        0.8,
        {14: 0, 15: 1},
    )
    other = along(send, ((0, 1, 0), (1, 0, 0)))
    grad, loss = call(
        final_kernel,
        (core, arrived, keep, other, losses),
        (shape(peers // 2, 2, per_peer, features, dtype=BF16), shape(1, rows)),
        0.01,
    )
    row_loss = lax.ppermute(
        loss, ("c", "zh"), [(c * 2 + h, h * 2 + c) for h in range(2) for c in range(2)]
    )
    row_loss = call(copy_kernel, (row_loss,), shape(1, rows), 0.001)
    sent_back = lax.all_to_all(
        grad.reshape(peers, per_peer, features), WHERE, 0, 0, tiled=True
    )
    return sent_back.reshape(rows, features), row_loss


def solution(mesh):
    dp, grp = mesh.devices.shape
    parts = Mesh(
        mesh.devices.reshape(dp // 8, 4, 2, grp // 2, 2), ("zl", "x", "c", "y", "zh")
    )
    placed = P(("zl", "x", "c", "y", "zh"), None)

    def step(embeddings, order):
        return on_device(embeddings, order)

    step = jax.shard_map(
        step, mesh=parts, in_specs=(placed, placed), out_specs=(placed, placed), check_vma=False
    )
    return step
```

profile of v0, /device:TPU:8, one launch (start us, length us, event | category | flops | bytes accessed | tf_op | source)
XLA Modules:
  0.0 138.2 jit_solution(16852561417558782833)
XLA Ops:
  0.6 18.3 %all-to-all-start = ((bf16[48,8,512]{2,1,0:T(8,128)(2,1)}), bf16[48,8,512]{2,1,0:T(8,128)(2,1)S(1)}, u32[]{:S(2)}, u32[]{:S(2)}) async-start(bf16[48,8,512]{2,1,0:T(8,128)(2,1)} %bitcast.8), calls=%async_computation | async-start | bytes 786432 | tf_op jit(solution)/shard_map/all_to_all | solution.py:273
  18.9 21.8 %all-to-all-done = bf16[48,8,512]{2,1,0:T(8,128)(2,1)S(1)} async-done(((bf16[48,8,512]{2,1,0:T(8,128)(2,1)}), bf16[48,8,512]{2,1,0:T(8,128)(2,1)S(1)}, u32[]{:S(2)}, u32[]{:S(2)}) %all-to-all-start) | async-done | bytes 393248 | tf_op jit(solution)/shard_map/all_to_all | solution.py:273
  40.7 0.3 shard_map.41
  41.0 3.5 %collective-permute-start = (bf16[192,512]{1,0:T(8,128)(2,1)S(1)}, bf16[192,512]{1,0:T(8,128)(2,1)S(1)}, u32[]{:S(2)}, u32[]{:S(2)}) collective-permute-start(bf16[192,512]{1,0:T(8,128)(2,1)S(1)} %get-tuple-element.19), channel_id=1, source_target_pairs={{0,2},{2,4},{4,6},{6,8},{8,10},{10,12},{12,14},{14,0},{16,30},{18,... | collective-permute-start | bytes 589832 | tf_op jit(solution)/shard_map/ppermute | solution.py:268
  44.5 1.9 %collective-permute-start.1 = (bf16[192,512]{1,0:T(8,128)(2,1)S(1)}, bf16[192,512]{1,0:T(8,128)(2,1)S(1)}, u32[]{:S(2)}, u32[]{:S(2)}) collective-permute-start(bf16[192,512]{1,0:T(8,128)(2,1)S(1)} %get-tuple-element.20), channel_id=1, source_target_pairs={{16,2},{18,4},{20,6},{22,8},{24,10},{26,12},{28,14},{30,0},{0,30},... | collective-permute-start | bytes 589832 | tf_op jit(solution)/shard_map/ppermute | solution.py:268
  46.4 2.1 %collective-permute-done.n1a_ref = bf16[192,512]{1,0:T(8,128)(2,1)S(1)} collective-permute-done((bf16[192,512]{1,0:T(8,128)(2,1)S(1)}, bf16[192,512]{1,0:T(8,128)(2,1)S(1)}, u32[]{:S(2)}, u32[]{:S(2)}) %collective-permute-start) | collective-permute-done | bytes 196640 | tf_op jit(solution)/shard_map/ppermute | solution.py:268
  48.6 2.9 %collective-permute-done.1.n2a_ref = bf16[192,512]{1,0:T(8,128)(2,1)S(1)} collective-permute-done((bf16[192,512]{1,0:T(8,128)(2,1)S(1)}, bf16[192,512]{1,0:T(8,128)(2,1)S(1)}, u32[]{:S(2)}, u32[]{:S(2)}) %collective-permute-start.1) | collective-permute-done | bytes 196640 | tf_op jit(solution)/shard_map/ppermute | solution.py:268
  51.5 0.1 shard_map.42
  51.6 2.0 %collective-permute-start.2 = (bf16[768,512]{1,0:T(8,128)(2,1)S(1)}, bf16[768,512]{1,0:T(8,128)(2,1)S(1)}, u32[]{:S(2)}, u32[]{:S(2)}) collective-permute-start(bf16[768,512]{1,0:T(8,128)(2,1)S(1)} %get-tuple-element.21), channel_id=1, source_target_pairs={{0,16},{2,18},{4,20},{6,22},{8,24},{10,26},{12,28},{14,30},{16,0},... | collective-permute-start | bytes 2359304 | tf_op jit(solution)/shard_map/ppermute | solution.py:268
  53.6 4.5 %collective-permute-start.5 = (bf16[384,512]{1,0:T(8,128)(2,1)S(1)}, bf16[384,512]{1,0:T(8,128)(2,1)S(1)}, u32[]{:S(2)}, u32[]{:S(2)}) collective-permute-start(bf16[384,512]{1,0:T(8,128)(2,1)S(1)} %get-tuple-element.22), channel_id=1, source_target_pairs={{0,2},{2,4},{4,6},{6,8},{8,10},{10,12},{12,14},{14,0},{16,30},{18,... | collective-permute-start | bytes 1179656 | tf_op jit(solution)/shard_map/ppermute | solution.py:268
  58.1 2.1 %collective-permute-start.4 = (bf16[192,512]{1,0:T(8,128)(2,1)S(1)}, bf16[192,512]{1,0:T(8,128)(2,1)S(1)}, u32[]{:S(2)}, u32[]{:S(2)}) collective-permute-start(bf16[192,512]{1,0:T(8,128)(2,1)S(1)} %get-tuple-element.19), channel_id=1, source_target_pairs={{16,2},{18,4},{20,6},{22,8},{24,10},{26,12},{28,14},{30,0},{0,30},... | collective-permute-start | bytes 589832 | tf_op jit(solution)/shard_map/ppermute | solution.py:268
  60.2 3.4 %collective-permute-start.3 = (bf16[192,512]{1,0:T(8,128)(2,1)S(1)}, bf16[192,512]{1,0:T(8,128)(2,1)S(1)}, u32[]{:S(2)}, u32[]{:S(2)}) collective-permute-start(bf16[192,512]{1,0:T(8,128)(2,1)S(1)} %get-tuple-element.20), channel_id=1, source_target_pairs={{0,2},{2,4},{4,6},{6,8},{8,10},{10,12},{12,14},{14,0},{16,30},{18,... | collective-permute-start | bytes 589832 | tf_op jit(solution)/shard_map/ppermute | solution.py:268
  63.6 1.3 collective-permute-start.6
  64.9 0.0 collective-permute-done.6.o0_ref
  65.0 15.5 %collective-permute-start.8 = (s32[1,384]{1,0:T(1,128)}, s32[1,384]{1,0:T(1,128)S(1)}, u32[]{:S(2)}, u32[]{:S(2)}) collective-permute-start(s32[1,384]{1,0:T(1,128)} %param.3), channel_id=1, source_target_pairs={{0,28},{2,30},{4,16},{6,18},{8,20},{10,22},{12,24},{14,26},{16,29}... | collective-permute-start | bytes 4616 | tf_op jit(solution)/shard_map/ppermute | solution.py:264
  80.5 1.5 %collective-permute-done.8.o2_ref = s32[1,384]{1,0:T(1,128)S(1)} collective-permute-done((s32[1,384]{1,0:T(1,128)}, s32[1,384]{1,0:T(1,128)S(1)}, u32[]{:S(2)}, u32[]{:S(2)}) %collective-permute-start.8) | collective-permute-done | bytes 1568 | tf_op jit(solution)/shard_map/ppermute | solution.py:264
  82.0 2.3 %collective-permute-start.7 = (s32[1,384]{1,0:T(1,128)}, s32[1,384]{1,0:T(1,128)S(1)}, u32[]{:S(2)}, u32[]{:S(2)}) collective-permute-start(s32[1,384]{1,0:T(1,128)} %param.3), channel_id=1, source_target_pairs={{1,0},{3,2},{5,4},{7,6},{9,8},{11,10},{13,12},{15,14},{17,1},{19,3... | collective-permute-start | bytes 4616 | tf_op jit(solution)/shard_map/ppermute | solution.py:264
  84.3 9.7 %collective-permute-done.7.o1_ref = s32[1,384]{1,0:T(1,128)S(1)} collective-permute-done((s32[1,384]{1,0:T(1,128)}, s32[1,384]{1,0:T(1,128)S(1)}, u32[]{:S(2)}, u32[]{:S(2)}) %collective-permute-start.7) | collective-permute-done | bytes 1568 | tf_op jit(solution)/shard_map/ppermute | solution.py:264
  93.9 0.8 shard_map.43.sign_ref
  94.7 0.0 collective-permute-done.4.n2b_ref
  94.7 0.0 collective-permute-done.3.n1b_ref
  94.8 3.3 %shard_map.44 = (f32[768,768]{1,0:T(8,128)S(1)}, f32[384,384]{1,0:T(8,128)S(1)}, f32[384,8]{1,0:T(8,128)S(1)}, f32[384,512]{1,0:T(8,128)S(1)}, f32[384,512]{1,0:T(8,128)S(1)}, /*index=5*/f32[392,512]{1,0:T(8,128)S(1)}) custom-call(s32[1]{0:T(128)} %bitcast.core_ref, bf16[384,512]{1,0:T(8,128)(2,1)S(1)} %get-tuple-element.18.own_ref, ...), custom_call_target="tpu_custom_call" | custom-call | flops 2000000000 | bytes 100000 | tf_op jit(solution)/shard_map/pallas_call | solution.py:236
  98.1 2.0 %shard_map.45 = (f32[384,512]{1,0:T(8,128)S(1)}, f32[392,512]{1,0:T(8,128)S(1)}, f32[1,384]{1,0:T(1,128)S(1)}) custom-call(s32[1]{0:T(128)} %bitcast.core_ref, bf16[384,512]{1,0:T(8,128)(2,1)S(1)} %get-tuple-element.18.own_ref, bf16[768,512]{1,0:T(8,128)(2,1)S(1)} %collective-permute-done.2.both_ref, ...), custom_call_target="tpu_custom_call", output_to_operand_aliasing={{0}: (14, {}), {1}: (15, {})} | custom-call | flops 800000000 | bytes 100000 | tf_op jit(solution)/shard_map/pallas_call | solution.py:236
  100.1 1.9 %collective-permute-start.9 = (f32[392,512]{1,0:T(8,128)S(1)}, f32[392,512]{1,0:T(8,128)S(1)}, u32[]{:S(2)}, u32[]{:S(2)}) collective-permute-start(f32[392,512]{1,0:T(8,128)S(1)} %get-tuple-element.30), channel_id=1, source_target_pairs={{0,16},{2,18},{4,20},{6,22},{8,24},{10,26},{12,28},{14,30},{16,0},... | collective-permute-start | bytes 2408456 | tf_op jit(solution)/shard_map/ppermute | solution.py:268
  102.0 2.3 %collective-permute-done.9.other_ref = f32[392,512]{1,0:T(8,128)S(1)} collective-permute-done((f32[392,512]{1,0:T(8,128)S(1)}, f32[392,512]{1,0:T(8,128)S(1)}, u32[]{:S(2)}, u32[]{:S(2)}) %collective-permute-start.9) | collective-permute-done | bytes 802848 | tf_op jit(solution)/shard_map/ppermute | solution.py:268
  104.3 1.1 shard_map.46
  105.4 9.7 %all-to-all-start.1 = ((bf16[48,8,512]{2,1,0:T(8,128)(2,1)}), bf16[48,8,512]{2,1,0:T(8,128)(2,1)S(1)}, u32[]{:S(2)}, u32[]{:S(2)}) async-start(bf16[48,8,512]{2,1,0:T(8,128)(2,1)} %bitcast.3), calls=%async_computation.1 | async-start | bytes 786432 | tf_op jit(solution)/shard_map/all_to_all | solution.py:325
  115.1 0.7 collective-permute-start.10
  115.7 0.0 collective-permute-done.10.x_ref
  115.7 0.6 shard_map.47
  116.3 21.1 %all-to-all-done.1 = bf16[48,8,512]{2,1,0:T(8,128)(2,1)S(1)} async-done(((bf16[48,8,512]{2,1,0:T(8,128)(2,1)}), bf16[48,8,512]{2,1,0:T(8,128)(2,1)S(1)}, u32[]{:S(2)}, u32[]{:S(2)}) %all-to-all-start.1) | async-done | bytes 393248 | tf_op jit(solution)/shard_map/all_to_all | solution.py:325
  137.4 0.7 copy.9
  (2 shorter events, 0.0 us)
Async XLA Ops:
  0.6 40.1 %all-to-all-start = ((bf16[48,8,512]{2,1,0:T(8,128)(2,1)}), bf16[48,8,512]{2,1,0:T(8,128)(2,1)S(1)}, u32[]{:S(2)}, u32[]{:S(2)}) async-start(bf16[48,8,512]{2,1,0:T(8,128)(2,1)} %bitcast.8), calls=%async_computation | async-start | bytes 786432 | tf_op jit(solution)/shard_map/all_to_all | solution.py:273
  41.0 7.6 %collective-permute-start = (bf16[192,512]{1,0:T(8,128)(2,1)S(1)}, bf16[192,512]{1,0:T(8,128)(2,1)S(1)}, u32[]{:S(2)}, u32[]{:S(2)}) collective-permute-start(bf16[192,512]{1,0:T(8,128)(2,1)S(1)} %get-tuple-element.19), channel_id=1, source_target_pairs={{0,2},{2,4},{4,6},{6,8},{8,10},{10,12},{12,14},{14,0},{16,30},{18,... | collective-permute-start | bytes 589832 | tf_op jit(solution)/shard_map/ppermute | solution.py:268
  44.5 7.0 %collective-permute-start.1 = (bf16[192,512]{1,0:T(8,128)(2,1)S(1)}, bf16[192,512]{1,0:T(8,128)(2,1)S(1)}, u32[]{:S(2)}, u32[]{:S(2)}) collective-permute-start(bf16[192,512]{1,0:T(8,128)(2,1)S(1)} %get-tuple-element.20), channel_id=1, source_target_pairs={{16,2},{18,4},{20,6},{22,8},{24,10},{26,12},{28,14},{30,0},{0,30},... | collective-permute-start | bytes 589832 | tf_op jit(solution)/shard_map/ppermute | solution.py:268
  51.6 43.2 %collective-permute-start.2 = (bf16[768,512]{1,0:T(8,128)(2,1)S(1)}, bf16[768,512]{1,0:T(8,128)(2,1)S(1)}, u32[]{:S(2)}, u32[]{:S(2)}) collective-permute-start(bf16[768,512]{1,0:T(8,128)(2,1)S(1)} %get-tuple-element.21), channel_id=1, source_target_pairs={{0,16},{2,18},{4,20},{6,22},{8,24},{10,26},{12,28},{14,30},{16,0},... | collective-permute-start | bytes 2359304 | tf_op jit(solution)/shard_map/ppermute | solution.py:268
  53.6 44.5 %collective-permute-start.5 = (bf16[384,512]{1,0:T(8,128)(2,1)S(1)}, bf16[384,512]{1,0:T(8,128)(2,1)S(1)}, u32[]{:S(2)}, u32[]{:S(2)}) collective-permute-start(bf16[384,512]{1,0:T(8,128)(2,1)S(1)} %get-tuple-element.22), channel_id=1, source_target_pairs={{0,2},{2,4},{4,6},{6,8},{8,10},{10,12},{12,14},{14,0},{16,30},{18,... | collective-permute-start | bytes 1179656 | tf_op jit(solution)/shard_map/ppermute | solution.py:268
  58.1 36.6 %collective-permute-start.4 = (bf16[192,512]{1,0:T(8,128)(2,1)S(1)}, bf16[192,512]{1,0:T(8,128)(2,1)S(1)}, u32[]{:S(2)}, u32[]{:S(2)}) collective-permute-start(bf16[192,512]{1,0:T(8,128)(2,1)S(1)} %get-tuple-element.19), channel_id=1, source_target_pairs={{16,2},{18,4},{20,6},{22,8},{24,10},{26,12},{28,14},{30,0},{0,30},... | collective-permute-start | bytes 589832 | tf_op jit(solution)/shard_map/ppermute | solution.py:268
  60.2 34.5 %collective-permute-start.3 = (bf16[192,512]{1,0:T(8,128)(2,1)S(1)}, bf16[192,512]{1,0:T(8,128)(2,1)S(1)}, u32[]{:S(2)}, u32[]{:S(2)}) collective-permute-start(bf16[192,512]{1,0:T(8,128)(2,1)S(1)} %get-tuple-element.20), channel_id=1, source_target_pairs={{0,2},{2,4},{4,6},{6,8},{8,10},{10,12},{12,14},{14,0},{16,30},{18,... | collective-permute-start | bytes 589832 | tf_op jit(solution)/shard_map/ppermute | solution.py:268
  63.6 1.3 collective-permute-start.6
  65.0 17.0 %collective-permute-start.8 = (s32[1,384]{1,0:T(1,128)}, s32[1,384]{1,0:T(1,128)S(1)}, u32[]{:S(2)}, u32[]{:S(2)}) collective-permute-start(s32[1,384]{1,0:T(1,128)} %param.3), channel_id=1, source_target_pairs={{0,28},{2,30},{4,16},{6,18},{8,20},{10,22},{12,24},{14,26},{16,29}... | collective-permute-start | bytes 4616 | tf_op jit(solution)/shard_map/ppermute | solution.py:264
  82.0 12.0 %collective-permute-start.7 = (s32[1,384]{1,0:T(1,128)}, s32[1,384]{1,0:T(1,128)S(1)}, u32[]{:S(2)}, u32[]{:S(2)}) collective-permute-start(s32[1,384]{1,0:T(1,128)} %param.3), channel_id=1, source_target_pairs={{1,0},{3,2},{5,4},{7,6},{9,8},{11,10},{13,12},{15,14},{17,1},{19,3... | collective-permute-start | bytes 4616 | tf_op jit(solution)/shard_map/ppermute | solution.py:264
  100.1 4.2 %collective-permute-start.9 = (f32[392,512]{1,0:T(8,128)S(1)}, f32[392,512]{1,0:T(8,128)S(1)}, u32[]{:S(2)}, u32[]{:S(2)}) collective-permute-start(f32[392,512]{1,0:T(8,128)S(1)} %get-tuple-element.30), channel_id=1, source_target_pairs={{0,16},{2,18},{4,20},{6,22},{8,24},{10,26},{12,28},{14,30},{16,0},... | collective-permute-start | bytes 2408456 | tf_op jit(solution)/shard_map/ppermute | solution.py:268
  105.4 32.1 %all-to-all-start.1 = ((bf16[48,8,512]{2,1,0:T(8,128)(2,1)}), bf16[48,8,512]{2,1,0:T(8,128)(2,1)S(1)}, u32[]{:S(2)}, u32[]{:S(2)}) async-start(bf16[48,8,512]{2,1,0:T(8,128)(2,1)} %bitcast.3), calls=%async_computation.1 | async-start | bytes 786432 | tf_op jit(solution)/shard_map/all_to_all | solution.py:325
  115.1 0.7 collective-permute-start.10
where the time goes:
time: 139 us; the launch traced here: 138 us
  starting transfers between devices  67.1 us (48%)
  waiting for transfers between devices  61.4 us (44%)
  Pallas kernels  8.06 us (6%)
    all_to_all x1, waiting for transfers between devices, on_device(): lax.all_to_all(embeddings.reshape(peers, per_peer, features), WHERE, 0, 0...  21.8 us
    all_to_all x1, waiting for transfers between devices, on_device(): lax.all_to_all(grad.reshape(peers, per_peer, features), WHERE, 0, 0, tile...  21.1 us
    ppermute x7, starting transfers between devices, along(): return lax.ppermute(value, ('c', 'y'), route)  19.3 us
    ppermute x3, starting transfers between devices, fetch_order(): return lax.ppermute(order, ('c', 'y', 'zh'), route)  19.1 us
    all_to_all x1, starting transfers between devices, on_device(): lax.all_to_all(embeddings.reshape(peers, per_peer, features), WHERE, 0, 0...  18.3 us
    ppermute x3, waiting for transfers between devices, fetch_order(): return lax.ppermute(order, ('c', 'y', 'zh'), route)  11.2 us
    all_to_all x1, starting transfers between devices, on_device(): lax.all_to_all(grad.reshape(peers, per_peer, features), WHERE, 0, 0, tile...  9.67 us
    pallas_call x7, Pallas kernels, call(): pl.pallas_call(kernel, out_shape=outputs, in_specs=[SMEM if a.ndim == 1 e...  8.06 us
  transfers between devices with their start and end apart: 13, of which 7 were waited for; matrix products, arithmetic and copies ran while one was open for 0% of the time, Pallas kernels for 3%

commit v1 on v0

--- a/solution.py
+++ b/solution.py
@@ -22,6 +22,10 @@
 def chip_rows(own, sib):
     half = own.shape[0] // 2
     return jnp.concatenate([own[0:half], sib[0:half], own[half:], sib[half:]], axis=0)
+
+
+def cols_by_cols(a, b):
+    return lax.dot_general(a, b, (((0,), (0,)), ((), ())), preferred_element_type=F32)
 
 
 def as_row(column):
@@ -140,15 +144,14 @@
         d_bb, pos, neg = signed_exp(sign, rows_by_rows(chip[b], chip[b]))
         neg_sum = over_columns(e_b) + over_columns(d_ba) + over_columns(neg)
         up, down, loss = factors(over_columns(pos), neg_sum)
-        row_up = as_row(up)
         send_ref[rows : rows + 1, 0:rows] = over_rows(jnp.where(arrived_rows(o1_ref), loss, 0.0))
-        coef = paired(sign, up, down, row_up, as_row(down), d_bb)
+        coef = paired(sign, up, down, as_row(up), as_row(down), d_bb)
         total = jnp.dot(coef, chip[b], preferred_element_type=F32)
-        total = total + scaled_dot(up, e_b, near) + scaled_dot(up, d_ba, chip[a])
+        coef_ba = (up * d_ba).astype(BF16)
+        acc_ref[...] = cols_by_cols(coef_ba, chip[b])
+        total = total + jnp.dot(coef_ba, chip[a], preferred_element_type=F32)
+        total = total + scaled_dot(up, e_b, near)
         split_store(1, total, keep_ref, send_ref)
-
-        d_ab = jnp.exp(gamma * rows_by_rows(chip[a], chip[b]))
-        acc_ref[...] = scaled_dot(row_up, d_ab, chip[b])
         e_a = jnp.exp(gamma * rows_by_rows(chip[a], near))
         e_ref[a] = e_a
         d_aa, pos, neg = signed_exp(sign_ref[0], rows_by_rows(chip[a], chip[a]))
@@ -174,7 +177,7 @@
 
 def late_kernel(
     core_ref, own_ref, both_ref, n1a_ref, n2a_ref, n1b_ref, n2b_ref, far_ref, sign_ref,
-    e_ref, d_ref, sums_ref, acc_ref, o0_ref, keep_in, send_in, keep_ref, send_ref, loss_ref,
+    e_ref, d_ref, sums_ref, acc_ref, keep_in, send_in, keep_ref, send_ref, loss_ref,
 ):
     core = core_ref[0]
     rows = own_ref.shape[0]
@@ -191,7 +194,7 @@
         total = acc_ref[...] + jnp.dot(coef, chip[a], preferred_element_type=F32)
         total = total + scaled_dot(up, e_ref[a], near) + scaled_dot(up, f, far)
         split_store(0, total, keep_ref, send_ref)
-        loss_ref[...] = over_rows(jnp.where(arrived_rows(o0_ref), loss, 0.0))
+        loss_ref[:, 0:1] = loss
 
     @pl.when(core == 1)
     def _():
@@ -200,23 +203,34 @@
         others = jnp.exp(gamma * rows_by_rows(near, far))
         up, _, _ = factors(over_rows(pos), over_rows(f) + over_rows(neg) + over_rows(others))
         split_store(1, acc_ref[...] + scaled_dot(up, f, far), keep_ref, send_ref)
-        loss_ref[...] = jnp.zeros_like(loss_ref)
-
-
-def final_kernel(core_ref, x_ref, keep_ref, other_ref, losses_ref, grad_ref, loss_ref):
-    rows = keep_ref.shape[0]
+
+
+def prepare_kernel(core_ref, x_ref, loss_col_ref, o0_ref, u_ref, inv_ref, loss_ref):
+    features = x_ref.shape[-1]
+    half = u_ref.shape[0] // 2
+    for which in range(2):
+        part = slice(which * half, (which + 1) * half)
+        x = x_ref[:, which].astype(F32).reshape(half, features)
+        inv = lax.rsqrt(jnp.sum(x * x, axis=1, keepdims=True) + 1e-06)
+        u_ref[part] = x * inv
+        inv_ref[part, 0:1] = inv
+
+    @pl.when(core_ref[0] == 0)
+    def _():
+        loss_ref[...] = over_rows(jnp.where(arrived_rows(o0_ref), loss_col_ref[:, 0:1], 0.0))
+
+
+def final_kernel(core_ref, u_ref, inv_ref, keep_ref, other_ref, losses_ref, grad_ref, loss_ref):
+    rows, features = keep_ref.shape
     loss_ref[...] = jnp.where(
         core_ref[0] == 0, losses_ref[...], other_ref[rows : rows + 1, 0:rows]
     )
-    features = x_ref.shape[-1]
-    half = keep_ref.shape[0] // 2
+    half = rows // 2
     for which in range(2):
         part = slice(which * half, (which + 1) * half)
         total = keep_ref[part] + other_ref[part]
-        x = x_ref[:, which].astype(F32).reshape(half, features)
-        inv = lax.rsqrt(jnp.sum(x * x, axis=1, keepdims=True) + 1e-06)
-        u = x * inv
-        grad = (total - u * jnp.sum(u * total, axis=1, keepdims=True)) * inv
+        u = u_ref[part]
+        grad = (total - u * jnp.sum(u * total, axis=1, keepdims=True)) * inv_ref[part, 0:1]
         grad_ref[:, which] = grad.reshape(half // 8, 8, features).astype(BF16)
 
 
@@ -304,17 +318,23 @@
         ),
         2.0,
     )
-    keep, send, losses = call(
+    keep, send, loss_col = call(
         late_kernel,
-        (core, own, sib, *near, far, sign, e, d, sums, acc, o0, keep, send),
-        (*half_grads, shape(1, rows)),
+        (core, own, sib, *near, far, sign, e, d, sums, acc, keep, send),
+        (*half_grads, shape(rows, 8)),
         0.8,
-        {14: 0, 15: 1},
+        {13: 0, 14: 1},
     )
     other = along(send, ((0, 1, 0), (1, 0, 0)))
+    u, inv, losses = call(
+        prepare_kernel,
+        (core, arrived, loss_col, o0),
+        (shape(rows, features), shape(rows, 8), shape(1, rows)),
+        0.01,
+    )
     grad, loss = call(
         final_kernel,
-        (core, arrived, keep, other, losses),
+        (core, u, inv, keep, other, losses),
         (shape(peers // 2, 2, per_peer, features, dtype=BF16), shape(1, rows)),
         0.01,
     )

time: 139 us -> 139 us (level)
    pallas_call x7 -> x8, Pallas kernels: 8.06 us -> 8.24 us  [call(): pl.pallas_call(kernel, out_shape=outputs, in_specs=[SMEM if a.ndim == 1 e...]
  transfers between devices with their start and end apart: 13 -> 13, of which waited for: 7 -> 7; matrix products, arithmetic and copies ran while one was open for 0% -> 0% of each run, Pallas kernels for 3% -> 4%
where the time goes in v1:
time: 139 us; the launch traced here: 138 us
  starting transfers between devices  67.3 us (48%)
  waiting for transfers between devices  61.1 us (44%)
  Pallas kernels  8.24 us (6%)
    all_to_all x1, waiting for transfers between devices, on_device(): lax.all_to_all(embeddings.reshape(peers, per_peer, features), WHERE, 0, 0...  21.8 us
    all_to_all x1, waiting for transfers between devices, on_device(): lax.all_to_all(grad.reshape(peers, per_peer, features), WHERE, 0, 0, tile...  21.1 us
    ppermute x7, starting transfers between devices, along(): return lax.ppermute(value, ('c', 'y'), route)  19.3 us
    ppermute x3, starting transfers between devices, fetch_order(): return lax.ppermute(order, ('c', 'y', 'zh'), route)  19.1 us
    all_to_all x1, starting transfers between devices, on_device(): lax.all_to_all(embeddings.reshape(peers, per_peer, features), WHERE, 0, 0...  18.3 us
    ppermute x3, waiting for transfers between devices, fetch_order(): return lax.ppermute(order, ('c', 'y', 'zh'), route)  11.2 us
    all_to_all x1, starting transfers between devices, on_device(): lax.all_to_all(grad.reshape(peers, per_peer, features), WHERE, 0, 0, tile...  9.81 us
    pallas_call x8, Pallas kernels, call(): pl.pallas_call(kernel, out_shape=outputs, in_specs=[SMEM if a.ndim == 1 e...  8.24 us
  transfers between devices with their start and end apart: 13, of which 7 were waited for; matrix products, arithmetic and copies ran while one was open for 0% of the time, Pallas kernels for 4%

profile of v1, /device:TPU:8, one launch (start us, length us, event | category | flops | bytes accessed | tf_op | source)
XLA Modules:
  0.0 138.2 jit_solution(12831675305827638043)
XLA Ops:
  0.6 18.3 %all-to-all-start = ((bf16[48,8,512]{2,1,0:T(8,128)(2,1)}), bf16[48,8,512]{2,1,0:T(8,128)(2,1)S(1)}, u32[]{:S(2)}, u32[]{:S(2)}) async-start(bf16[48,8,512]{2,1,0:T(8,128)(2,1)} %bitcast.8), calls=%async_computation | async-start | bytes 786432 | tf_op jit(solution)/shard_map/all_to_all | solution.py:287
  18.9 21.8 %all-to-all-done = bf16[48,8,512]{2,1,0:T(8,128)(2,1)S(1)} async-done(((bf16[48,8,512]{2,1,0:T(8,128)(2,1)}), bf16[48,8,512]{2,1,0:T(8,128)(2,1)S(1)}, u32[]{:S(2)}, u32[]{:S(2)}) %all-to-all-start) | async-done | bytes 393248 | tf_op jit(solution)/shard_map/all_to_all | solution.py:287
  40.7 0.3 shard_map.41
  41.0 3.5 %collective-permute-start = (bf16[192,512]{1,0:T(8,128)(2,1)S(1)}, bf16[192,512]{1,0:T(8,128)(2,1)S(1)}, u32[]{:S(2)}, u32[]{:S(2)}) collective-permute-start(bf16[192,512]{1,0:T(8,128)(2,1)S(1)} %get-tuple-element.22), channel_id=1, source_target_pairs={{0,2},{2,4},{4,6},{6,8},{8,10},{10,12},{12,14},{14,0},{16,30},{18,... | collective-permute-start | bytes 589832 | tf_op jit(solution)/shard_map/ppermute | solution.py:282
  44.5 1.9 %collective-permute-start.1 = (bf16[192,512]{1,0:T(8,128)(2,1)S(1)}, bf16[192,512]{1,0:T(8,128)(2,1)S(1)}, u32[]{:S(2)}, u32[]{:S(2)}) collective-permute-start(bf16[192,512]{1,0:T(8,128)(2,1)S(1)} %get-tuple-element.23), channel_id=1, source_target_pairs={{16,2},{18,4},{20,6},{22,8},{24,10},{26,12},{28,14},{30,0},{0,30},... | collective-permute-start | bytes 589832 | tf_op jit(solution)/shard_map/ppermute | solution.py:282
  46.4 2.1 %collective-permute-done.n1a_ref = bf16[192,512]{1,0:T(8,128)(2,1)S(1)} collective-permute-done((bf16[192,512]{1,0:T(8,128)(2,1)S(1)}, bf16[192,512]{1,0:T(8,128)(2,1)S(1)}, u32[]{:S(2)}, u32[]{:S(2)}) %collective-permute-start) | collective-permute-done | bytes 196640 | tf_op jit(solution)/shard_map/ppermute | solution.py:282
  48.6 2.9 %collective-permute-done.1.n2a_ref = bf16[192,512]{1,0:T(8,128)(2,1)S(1)} collective-permute-done((bf16[192,512]{1,0:T(8,128)(2,1)S(1)}, bf16[192,512]{1,0:T(8,128)(2,1)S(1)}, u32[]{:S(2)}, u32[]{:S(2)}) %collective-permute-start.1) | collective-permute-done | bytes 196640 | tf_op jit(solution)/shard_map/ppermute | solution.py:282
  51.5 0.1 shard_map.42
  51.6 2.0 %collective-permute-start.2 = (bf16[768,512]{1,0:T(8,128)(2,1)S(1)}, bf16[768,512]{1,0:T(8,128)(2,1)S(1)}, u32[]{:S(2)}, u32[]{:S(2)}) collective-permute-start(bf16[768,512]{1,0:T(8,128)(2,1)S(1)} %get-tuple-element.24), channel_id=1, source_target_pairs={{0,16},{2,18},{4,20},{6,22},{8,24},{10,26},{12,28},{14,30},{16,0},... | collective-permute-start | bytes 2359304 | tf_op jit(solution)/shard_map/ppermute | solution.py:282
  53.6 4.5 %collective-permute-start.5 = (bf16[384,512]{1,0:T(8,128)(2,1)S(1)}, bf16[384,512]{1,0:T(8,128)(2,1)S(1)}, u32[]{:S(2)}, u32[]{:S(2)}) collective-permute-start(bf16[384,512]{1,0:T(8,128)(2,1)S(1)} %get-tuple-element.25), channel_id=1, source_target_pairs={{0,2},{2,4},{4,6},{6,8},{8,10},{10,12},{12,14},{14,0},{16,30},{18,... | collective-permute-start | bytes 1179656 | tf_op jit(solution)/shard_map/ppermute | solution.py:282
  58.1 2.1 %collective-permute-start.4 = (bf16[192,512]{1,0:T(8,128)(2,1)S(1)}, bf16[192,512]{1,0:T(8,128)(2,1)S(1)}, u32[]{:S(2)}, u32[]{:S(2)}) collective-permute-start(bf16[192,512]{1,0:T(8,128)(2,1)S(1)} %get-tuple-element.22), channel_id=1, source_target_pairs={{16,2},{18,4},{20,6},{22,8},{24,10},{26,12},{28,14},{30,0},{0,30},... | collective-permute-start | bytes 589832 | tf_op jit(solution)/shard_map/ppermute | solution.py:282
  60.2 3.4 %collective-permute-start.3 = (bf16[192,512]{1,0:T(8,128)(2,1)S(1)}, bf16[192,512]{1,0:T(8,128)(2,1)S(1)}, u32[]{:S(2)}, u32[]{:S(2)}) collective-permute-start(bf16[192,512]{1,0:T(8,128)(2,1)S(1)} %get-tuple-element.23), channel_id=1, source_target_pairs={{0,2},{2,4},{4,6},{6,8},{8,10},{10,12},{12,14},{14,0},{16,30},{18,... | collective-permute-start | bytes 589832 | tf_op jit(solution)/shard_map/ppermute | solution.py:282
  63.6 1.3 collective-permute-start.6
  65.0 15.5 %collective-permute-start.8 = (s32[1,384]{1,0:T(1,128)}, s32[1,384]{1,0:T(1,128)S(1)}, u32[]{:S(2)}, u32[]{:S(2)}) collective-permute-start(s32[1,384]{1,0:T(1,128)} %param.3), channel_id=1, source_target_pairs={{0,28},{2,30},{4,16},{6,18},{8,20},{10,22},{12,24},{14,26},{16,29}... | collective-permute-start | bytes 4616 | tf_op jit(solution)/shard_map/ppermute | solution.py:278
  80.5 1.5 %collective-permute-done.8.o2_ref = s32[1,384]{1,0:T(1,128)S(1)} collective-permute-done((s32[1,384]{1,0:T(1,128)}, s32[1,384]{1,0:T(1,128)S(1)}, u32[]{:S(2)}, u32[]{:S(2)}) %collective-permute-start.8) | collective-permute-done | bytes 1568 | tf_op jit(solution)/shard_map/ppermute | solution.py:278
  82.0 2.3 %collective-permute-start.7 = (s32[1,384]{1,0:T(1,128)}, s32[1,384]{1,0:T(1,128)S(1)}, u32[]{:S(2)}, u32[]{:S(2)}) collective-permute-start(s32[1,384]{1,0:T(1,128)} %param.3), channel_id=1, source_target_pairs={{1,0},{3,2},{5,4},{7,6},{9,8},{11,10},{13,12},{15,14},{17,1},{19,3... | collective-permute-start | bytes 4616 | tf_op jit(solution)/shard_map/ppermute | solution.py:278
  84.3 9.7 %collective-permute-done.7.o1_ref = s32[1,384]{1,0:T(1,128)S(1)} collective-permute-done((s32[1,384]{1,0:T(1,128)}, s32[1,384]{1,0:T(1,128)S(1)}, u32[]{:S(2)}, u32[]{:S(2)}) %collective-permute-start.7) | collective-permute-done | bytes 1568 | tf_op jit(solution)/shard_map/ppermute | solution.py:278
  93.9 0.8 shard_map.43.sign_ref
  94.7 0.0 collective-permute-done.4.n2b_ref
  94.7 0.0 collective-permute-done.3.n1b_ref
  94.8 3.2 %shard_map.44 = (f32[768,768]{1,0:T(8,128)S(1)}, f32[384,384]{1,0:T(8,128)S(1)}, f32[384,8]{1,0:T(8,128)S(1)}, f32[384,512]{1,0:T(8,128)S(1)}, f32[384,512]{1,0:T(8,128)S(1)}, /*index=5*/f32[392,512]{1,0:T(8,128)S(1)}) custom-call(s32[1]{0:T(128)} %bitcast.core_ref, bf16[384,512]{1,0:T(8,128)(2,1)S(1)} %get-tuple-element.21.own_ref, ...), custom_call_target="tpu_custom_call" | custom-call | flops 2000000000 | bytes 100000 | tf_op jit(solution)/shard_map/pallas_call | solution.py:250
  98.0 0.0 collective-permute-done.5.far_ref
  98.0 2.0 %shard_map.45 = (f32[384,512]{1,0:T(8,128)S(1)}, f32[392,512]{1,0:T(8,128)S(1)}, f32[384,8]{1,0:T(8,128)S(1)}) custom-call(s32[1]{0:T(128)} %bitcast.core_ref, bf16[384,512]{1,0:T(8,128)(2,1)S(1)} %get-tuple-element.21.own_ref, bf16[768,512]{1,0:T(8,128)(2,1)S(1)} %collective-permute-done.2.both_ref, ...), custom_call_target="tpu_custom_call", output_to_operand_aliasing={{0}: (13, {}), {1}: (14, {})} | custom-call | flops 800000000 | bytes 100000 | tf_op jit(solution)/shard_map/pallas_call | solution.py:250
  100.0 1.9 %collective-permute-start.9 = (f32[392,512]{1,0:T(8,128)S(1)}, f32[392,512]{1,0:T(8,128)S(1)}, u32[]{:S(2)}, u32[]{:S(2)}) collective-permute-start(f32[392,512]{1,0:T(8,128)S(1)} %get-tuple-element.36), channel_id=1, source_target_pairs={{0,16},{2,18},{4,20},{6,22},{8,24},{10,26},{12,28},{14,30},{16,0},... | collective-permute-start | bytes 2408456 | tf_op jit(solution)/shard_map/ppermute | solution.py:282
  101.9 0.3 shard_map.46
  102.2 2.0 %collective-permute-done.9.other_ref = f32[392,512]{1,0:T(8,128)S(1)} collective-permute-done((f32[392,512]{1,0:T(8,128)S(1)}, f32[392,512]{1,0:T(8,128)S(1)}, u32[]{:S(2)}, u32[]{:S(2)}) %collective-permute-start.9) | collective-permute-done | bytes 802848 | tf_op jit(solution)/shard_map/ppermute | solution.py:282
  104.2 1.1 shard_map.47
  105.2 9.8 %all-to-all-start.1 = ((bf16[48,8,512]{2,1,0:T(8,128)(2,1)}), bf16[48,8,512]{2,1,0:T(8,128)(2,1)S(1)}, u32[]{:S(2)}, u32[]{:S(2)}) async-start(bf16[48,8,512]{2,1,0:T(8,128)(2,1)} %bitcast.3), calls=%async_computation.1 | async-start | bytes 786432 | tf_op jit(solution)/shard_map/all_to_all | solution.py:345
  115.1 0.7 collective-permute-start.10
  115.7 0.6 shard_map.48
  116.3 21.1 %all-to-all-done.1 = bf16[48,8,512]{2,1,0:T(8,128)(2,1)S(1)} async-done(((bf16[48,8,512]{2,1,0:T(8,128)(2,1)}), bf16[48,8,512]{2,1,0:T(8,128)(2,1)S(1)}, u32[]{:S(2)}, u32[]{:S(2)}) %all-to-all-start.1) | async-done | bytes 393248 | tf_op jit(solution)/shard_map/all_to_all | solution.py:345
  137.4 0.7 copy.9
  (3 shorter events, 0.0 us)
Async XLA Ops:
  0.6 40.1 %all-to-all-start = ((bf16[48,8,512]{2,1,0:T(8,128)(2,1)}), bf16[48,8,512]{2,1,0:T(8,128)(2,1)S(1)}, u32[]{:S(2)}, u32[]{:S(2)}) async-start(bf16[48,8,512]{2,1,0:T(8,128)(2,1)} %bitcast.8), calls=%async_computation | async-start | bytes 786432 | tf_op jit(solution)/shard_map/all_to_all | solution.py:287
  41.0 7.6 %collective-permute-start = (bf16[192,512]{1,0:T(8,128)(2,1)S(1)}, bf16[192,512]{1,0:T(8,128)(2,1)S(1)}, u32[]{:S(2)}, u32[]{:S(2)}) collective-permute-start(bf16[192,512]{1,0:T(8,128)(2,1)S(1)} %get-tuple-element.22), channel_id=1, source_target_pairs={{0,2},{2,4},{4,6},{6,8},{8,10},{10,12},{12,14},{14,0},{16,30},{18,... | collective-permute-start | bytes 589832 | tf_op jit(solution)/shard_map/ppermute | solution.py:282
  44.5 7.0 %collective-permute-start.1 = (bf16[192,512]{1,0:T(8,128)(2,1)S(1)}, bf16[192,512]{1,0:T(8,128)(2,1)S(1)}, u32[]{:S(2)}, u32[]{:S(2)}) collective-permute-start(bf16[192,512]{1,0:T(8,128)(2,1)S(1)} %get-tuple-element.23), channel_id=1, source_target_pairs={{16,2},{18,4},{20,6},{22,8},{24,10},{26,12},{28,14},{30,0},{0,30},... | collective-permute-start | bytes 589832 | tf_op jit(solution)/shard_map/ppermute | solution.py:282
  51.6 43.2 %collective-permute-start.2 = (bf16[768,512]{1,0:T(8,128)(2,1)S(1)}, bf16[768,512]{1,0:T(8,128)(2,1)S(1)}, u32[]{:S(2)}, u32[]{:S(2)}) collective-permute-start(bf16[768,512]{1,0:T(8,128)(2,1)S(1)} %get-tuple-element.24), channel_id=1, source_target_pairs={{0,16},{2,18},{4,20},{6,22},{8,24},{10,26},{12,28},{14,30},{16,0},... | collective-permute-start | bytes 2359304 | tf_op jit(solution)/shard_map/ppermute | solution.py:282
  53.6 44.4 %collective-permute-start.5 = (bf16[384,512]{1,0:T(8,128)(2,1)S(1)}, bf16[384,512]{1,0:T(8,128)(2,1)S(1)}, u32[]{:S(2)}, u32[]{:S(2)}) collective-permute-start(bf16[384,512]{1,0:T(8,128)(2,1)S(1)} %get-tuple-element.25), channel_id=1, source_target_pairs={{0,2},{2,4},{4,6},{6,8},{8,10},{10,12},{12,14},{14,0},{16,30},{18,... | collective-permute-start | bytes 1179656 | tf_op jit(solution)/shard_map/ppermute | solution.py:282
  58.1 36.6 %collective-permute-start.4 = (bf16[192,512]{1,0:T(8,128)(2,1)S(1)}, bf16[192,512]{1,0:T(8,128)(2,1)S(1)}, u32[]{:S(2)}, u32[]{:S(2)}) collective-permute-start(bf16[192,512]{1,0:T(8,128)(2,1)S(1)} %get-tuple-element.22), channel_id=1, source_target_pairs={{16,2},{18,4},{20,6},{22,8},{24,10},{26,12},{28,14},{30,0},{0,30},... | collective-permute-start | bytes 589832 | tf_op jit(solution)/shard_map/ppermute | solution.py:282
  60.2 34.5 %collective-permute-start.3 = (bf16[192,512]{1,0:T(8,128)(2,1)S(1)}, bf16[192,512]{1,0:T(8,128)(2,1)S(1)}, u32[]{:S(2)}, u32[]{:S(2)}) collective-permute-start(bf16[192,512]{1,0:T(8,128)(2,1)S(1)} %get-tuple-element.23), channel_id=1, source_target_pairs={{0,2},{2,4},{4,6},{6,8},{8,10},{10,12},{12,14},{14,0},{16,30},{18,... | collective-permute-start | bytes 589832 | tf_op jit(solution)/shard_map/ppermute | solution.py:282
  63.6 1.3 collective-permute-start.6
  65.0 17.0 %collective-permute-start.8 = (s32[1,384]{1,0:T(1,128)}, s32[1,384]{1,0:T(1,128)S(1)}, u32[]{:S(2)}, u32[]{:S(2)}) collective-permute-start(s32[1,384]{1,0:T(1,128)} %param.3), channel_id=1, source_target_pairs={{0,28},{2,30},{4,16},{6,18},{8,20},{10,22},{12,24},{14,26},{16,29}... | collective-permute-start | bytes 4616 | tf_op jit(solution)/shard_map/ppermute | solution.py:278
  82.0 12.0 %collective-permute-start.7 = (s32[1,384]{1,0:T(1,128)}, s32[1,384]{1,0:T(1,128)S(1)}, u32[]{:S(2)}, u32[]{:S(2)}) collective-permute-start(s32[1,384]{1,0:T(1,128)} %param.3), channel_id=1, source_target_pairs={{1,0},{3,2},{5,4},{7,6},{9,8},{11,10},{13,12},{15,14},{17,1},{19,3... | collective-permute-start | bytes 4616 | tf_op jit(solution)/shard_map/ppermute | solution.py:278
  100.0 4.2 %collective-permute-start.9 = (f32[392,512]{1,0:T(8,128)S(1)}, f32[392,512]{1,0:T(8,128)S(1)}, u32[]{:S(2)}, u32[]{:S(2)}) collective-permute-start(f32[392,512]{1,0:T(8,128)S(1)} %get-tuple-element.36), channel_id=1, source_target_pairs={{0,16},{2,18},{4,20},{6,22},{8,24},{10,26},{12,28},{14,30},{16,0},... | collective-permute-start | bytes 2408456 | tf_op jit(solution)/shard_map/ppermute | solution.py:282
  105.2 32.2 %all-to-all-start.1 = ((bf16[48,8,512]{2,1,0:T(8,128)(2,1)}), bf16[48,8,512]{2,1,0:T(8,128)(2,1)S(1)}, u32[]{:S(2)}, u32[]{:S(2)}) async-start(bf16[48,8,512]{2,1,0:T(8,128)(2,1)} %bitcast.3), calls=%async_computation.1 | async-start | bytes 786432 | tf_op jit(solution)/shard_map/all_to_all | solution.py:345
  115.1 0.7 collective-permute-start.10
